TPU v7x, 256 devices: a whole 4x4x8 slice. The times are simulated.
256 devices in a mesh: seq: 32 (over z, y), mp: 4 (over x), req: 2 (over core).
Axes of the slice: x: 4, y: 4, z: 8, core: 2. Of those that a mesh axis runs over, the one named last changes fastest.
Arguments:
- hidden: bfloat16 [2, 8192, 3072], P('req', 'seq', 'mp'), may hold values from -6 to 6
- norm_gain: bfloat16 [3072], replicated, may hold values from 0.5 to 1.5
- w_query: bfloat16 [3072, 1024], P(None, 'mp'), may hold values from -0.109375 to 0.109375
- w_keyval: bfloat16 [3072, 512], P(None, 'mp'), may hold values from -0.109375 to 0.109375
- w_attn_out: bfloat16 [1024, 3072], P('mp'), may hold values from -1.5 to 1.5
- w_inner: bfloat16 [3072, 2, 1536], P(None, None, 'mp'), may hold values from -0.109375 to 0.109375
- w_bc: bfloat16 [3072, 512], P(None, 'mp'), may hold values from -0.109375 to 0.109375
- w_dt: bfloat16 [3072, 12], P(None, 'mp'), may hold values from -0.109375 to 0.109375
- dt_bias: float32 [12], P('mp'), may hold values from -4 to 0
- a_log: float32 [12], P('mp'), may hold values from -12 to 0
- d_skip: float32 [12], P('mp'), may hold values from 0.1 to 10
- conv_x: bfloat16 [4, 1536], P(None, 'mp'), may hold values from -3 to 3
- conv_bc: bfloat16 [4, 512], replicated, may hold values from -3 to 3
- mamba_gain: bfloat16 [1536], P('mp'), may hold values from 0.5 to 1.5
- w_mamba_out: bfloat16 [1536, 3072], P('mp'), may hold values from -0.15625 to 0.15625
- cache: bfloat16 [2, 8192, 512], P('req', 'seq', 'mp'), may hold values from -70 to 70, as said below
- cache_len: int32 [2], P('req'), may hold values from 256 to 8192
- tail_x: bfloat16 [2, 3, 1536], P('req', None, 'mp'), may hold values from -6 to 6
- tail_bc: bfloat16 [2, 3, 512], P('req'), may hold values from -6 to 6
- ssm_init: float32 [2, 12, 128, 256], P('req', 'mp'), may hold values from -6 to 6
Outputs:
- layer_out: bfloat16 [2, 8192, 3072], P('req', 'seq', 'mp')
- new_keyval: bfloat16 [2, 8192, 512], P('req', 'seq', 'mp')
- block_states: float32 [2, 32, 12, 128, 256], P('req', 'seq', 'mp')
Inputs may be any that keep to these rules, and one draw needn't show every extreme that they name: Rows of the cache at or past cache_len are unused.
All inputs are finite; a program needn't handle non-finite values.
Results may differ from a plain program's by a relative error of at most 0.0097.
Values may be sent and summed in bfloat16 or wider, within the bound.
A program may use at most 192 MiB of HBM per device.

v0:
```python
import jax
import jax.numpy as jnp
from jax import lax
from jax.sharding import PartitionSpec as P

HD = 128
QH = 8
KVH = 2
NS = 256
CONV = 4
epsilon = 1e-05
rope_base = 100000000000.0
negative = -1e30


def shifted(block, axis, distance):
    devices = range(lax.axis_size(axis))
    route = [(i - distance, i) for i in devices if i - distance in devices]
    return lax.ppermute(block, axis, route)


def prefix(part, axis, combine, identity):
    place = lax.axis_index(axis)
    gathered = jax.tree.map(lambda a: lax.all_gather(a, axis), part)
    state = jax.tree.map(lambda a, e: jnp.zeros_like(a) + jnp.asarray(e, a.dtype), part, identity)

    def one(turn, state):
        return combine(
            state, jax.tree.map(lambda a: lax.dynamic_index_in_dim(a, turn, 0, False), gathered)
        )

    return lax.fori_loop(0, place, one, state)


def rotate(values, positions):
    half = HD // 2
    freqs = rope_base ** (-jnp.arange(half, dtype=jnp.float32) * 2.0 / HD)
    angles = positions.astype(jnp.float32)[:, None] * freqs[None, :]
    cosine = jnp.cos(angles)[:, None, :]
    sine = jnp.sin(angles)[:, None, :]
    first = values[..., :half]
    second = values[..., half:]
    return jnp.concatenate(
        [first * cosine - second * sine, second * cosine + first * sine], axis=-1
    )


def rms_scale(values):
    mean_sq = jnp.mean(values * values, axis=-1, keepdims=True)
    return values * lax.rsqrt(mean_sq + epsilon)


def causal_conv(tail, inputs, taps):
    padded = jnp.concatenate([tail, inputs], axis=0).astype(jnp.float32)
    count = inputs.shape[0]
    total = jnp.zeros(inputs.shape, jnp.float32)
    for offset in range(CONV):
        total = total + taps[offset].astype(jnp.float32)[None, :] * padded[offset : offset + count]
    return jax.nn.silu(total)


def join_states(earlier, later):
    return (earlier[0] * later[0], later[0][:, None, None] * earlier[1] + later[1])


def shards(
    hidden,
    norm_gain,
    w_query,
    w_keyval,
    w_attn_out,
    w_inner,
    w_bc,
    w_dt,
    dt_bias,
    a_log,
    d_skip,
    conv_x,
    conv_bc,
    mamba_gain,
    w_mamba_out,
    cache,
    cache_len,
    tail_x,
    tail_bc,
    ssm_init,
):
    high = lax.Precision.HIGHEST
    own_rows = hidden[0]
    tokens = own_rows.shape[0]
    seq_pos = lax.axis_index("seq")
    mp_pos = lax.axis_index("mp")
    length = cache_len[0]
    whole = lax.all_gather(own_rows, "mp", axis=1, tiled=True)
    normed = (rms_scale(whole.astype(jnp.float32)) * norm_gain.astype(jnp.float32)).astype(
        jnp.bfloat16
    )
    positions = length + seq_pos * tokens + jnp.arange(tokens, dtype=jnp.int32)
    local_heads = w_query.shape[1] // HD
    query = rotate(
        jnp.dot(normed, w_query, preferred_element_type=jnp.float32).reshape(
            tokens, local_heads, HD
        ),
        positions,
    ).astype(jnp.bfloat16)
    projected = jnp.dot(normed, w_keyval, preferred_element_type=jnp.float32)
    roped = rotate(projected[:, None, :], positions)[:, 0, :]
    kv_block = jnp.where(mp_pos % 2 == 0, roped, projected).astype(jnp.bfloat16)
    bc_block = jnp.dot(normed, w_bc, preferred_element_type=jnp.float32).astype(jnp.bfloat16)
    bc_all = lax.all_gather(bc_block, "mp", axis=1, tiled=True)
    mp_size = lax.axis_size("mp")
    pairs_of = [(i, i ^ 1) for i in range(mp_size)]
    is_key_block = mp_pos % 2 == 0

    def paired(own):
        other = lax.ppermute(own, "mp", pairs_of)
        return jnp.where(
            is_key_block,
            jnp.concatenate([own, other], axis=1),
            jnp.concatenate([other, own], axis=1),
        )

    cache_all = lax.all_gather(paired(cache[0]), "seq", axis=0, tiled=True)
    new_all = lax.all_gather(paired(kv_block), "seq", axis=0, tiled=True)
    inner = jnp.einsum("td,dkc->tkc", normed, w_inner, preferred_element_type=jnp.float32).astype(
        jnp.bfloat16
    )
    rim = CONV - 1
    prev_x, prev_bc = shifted((inner[tokens - rim :, 1], bc_all[tokens - rim :]), "seq", 1)
    first_block = seq_pos == 0
    prev_x = jnp.where(first_block, tail_x[0], prev_x)
    prev_bc = jnp.where(first_block, tail_bc[0], prev_bc)
    mamba_heads = dt_bias.shape[0]
    x_conv = causal_conv(prev_x, inner[:, 1], conv_x).reshape(tokens, mamba_heads, HD)
    bc_conv = causal_conv(prev_bc, bc_all, conv_bc)
    b_mat = bc_conv[:, :NS]
    c_mat = bc_conv[:, NS:]
    step_size = jax.nn.softplus(jnp.dot(normed, w_dt, preferred_element_type=jnp.float32) + dt_bias)
    log_decay = -step_size * jnp.exp(a_log)[None, :]
    cumulative = jnp.cumsum(log_decay, axis=0)
    pairs = jnp.dot(c_mat, b_mat.T, precision=high)
    gap = cumulative[:, None, :] - cumulative[None, :, :]
    token_ids = jnp.arange(tokens)
    lower = (token_ids[:, None] >= token_ids[None, :])[:, :, None]
    decay = jnp.where(lower, jnp.exp(jnp.where(lower, gap, 0.0)), 0.0)
    mixing = decay * pairs[:, :, None] * step_size[None, :, :]
    inner_out = jnp.einsum("tsh,shp->thp", mixing, x_conv, precision=high)
    to_end = jnp.exp(cumulative[-1][None, :] - cumulative) * step_size
    own_state = jnp.einsum("sh,shp,sn->hpn", to_end, x_conv, b_mat, precision=high)
    block_decay = jnp.exp(cumulative[-1])
    seq_size = lax.axis_size("seq")
    rows = HD // seq_size
    pieces = jnp.transpose(own_state.reshape(mamba_heads, seq_size, rows, NS), (1, 0, 2, 3))
    decays = jnp.broadcast_to(block_decay[None, :, None, None], (seq_size, mamba_heads, 1, NS))
    columns = lax.all_to_all(jnp.concatenate([pieces, decays], axis=2), "seq", 0, 0, tiled=True)
    carry = lax.dynamic_slice_in_dim(ssm_init[0], seq_pos * rows, rows, 1)
    entering = []
    for source in range(seq_size):
        entering.append(carry)
        part = columns[source]
        carry = part[:, rows:, :] * carry + part[:, :rows, :]
    entering = lax.all_to_all(jnp.stack(entering, axis=0), "seq", 0, 0, tiled=True)
    incoming = jnp.transpose(entering, (1, 0, 2, 3)).reshape(mamba_heads, HD, NS)
    carried = jnp.exp(cumulative)[:, :, None] * jnp.einsum(
        "tn,hpn->thp", c_mat, incoming, precision=high
    )
    mamba_y = inner_out + carried + d_skip[None, :, None] * x_conv
    state_after = block_decay[:, None, None] * incoming + own_state
    gated = mamba_y * jax.nn.silu(inner[:, 0].astype(jnp.float32).reshape(tokens, mamba_heads, HD))
    mixed = (
        rms_scale(gated).reshape(tokens, mamba_heads * HD) * mamba_gain.astype(jnp.float32)
    ).astype(jnp.bfloat16)
    cache_rows = cache.shape[1]
    shard_rows = cache_rows + tokens
    group = mp_pos * local_heads // (QH // KVH)
    query_index = seq_pos * tokens + jnp.arange(tokens, dtype=jnp.int32)
    scale = 1.0 / float(HD) ** 0.5
    piece = jnp.concatenate([cache_all, new_all], axis=0)
    top = jnp.full((local_heads, tokens), negative, jnp.float32)
    total_cache = cache_all.shape[0]
    index = jnp.arange(piece.shape[0], dtype=jnp.int32)
    in_cache = index < total_cache
    slot_ok = in_cache & (index < length)
    new_index = index - total_cache
    valid = slot_ok[None, :] | (~in_cache)[None, :] & (new_index[None, :] <= query_index[:, None])
    scores = (
        jnp.einsum("qhd,kd->hqk", query, piece[:, :HD], preferred_element_type=jnp.float32) * scale
    )
    masked = jnp.where(valid[None], scores, negative)
    new_top = jnp.maximum(top, jnp.max(masked, axis=-1))
    weights = jnp.where(valid[None], jnp.exp(masked - new_top[:, :, None]), 0.0)
    total = jnp.sum(weights, axis=-1)
    accum = jnp.einsum(
        "hqk,kd->hqd",
        weights.astype(jnp.bfloat16),
        piece[:, HD : 2 * HD],
        preferred_element_type=jnp.float32,
    )
    top, total, accum = (new_top, total, accum)
    attended = jnp.transpose(accum / total[:, :, None], (1, 0, 2)).reshape(tokens, local_heads * HD)
    attended = attended.astype(jnp.bfloat16)
    term = jnp.dot(attended, w_attn_out, preferred_element_type=jnp.float32)
    term = term + jnp.dot(mixed, w_mamba_out, preferred_element_type=jnp.float32)
    summed = lax.psum_scatter(term, "mp", scatter_dimension=1, tiled=True)
    layer = (summed + own_rows.astype(jnp.float32)).astype(jnp.bfloat16)
    return (layer[None], kv_block[None], state_after[None, None])


def solution(mesh):
    placed = (
        P("req", "seq", "mp"),
        P(),
        P(None, "mp"),
        P(None, "mp"),
        P("mp", None),
        P(None, None, "mp"),
        P(None, "mp"),
        P(None, "mp"),
        P("mp"),
        P("mp"),
        P("mp"),
        P(None, "mp"),
        P(),
        P("mp"),
        P("mp", None),
        P("req", "seq", "mp"),
        P("req"),
        P("req", None, "mp"),
        P("req", None, None),
        P("req", "mp", None, None),
    )
    return jax.shard_map(
        shards,
        mesh=mesh,
        in_specs=placed,
        out_specs=(P("req", "seq", "mp"), P("req", "seq", "mp"), P("req", "seq", "mp", None, None)),
        check_vma=False,
    )
```

profile of v0, /device:TPU:1, one launch (start us, length us, event | category | flops | bytes accessed | tf_op | source)
XLA Modules:
  0.0 330.6 jit_solution(8155268910153722102)
XLA Ops:
  8.9 2.1 collective-permute-start
  18.8 15.6 %and_or_fusion = pred[256,16384]{0,1:T(8,128)(4,1)} fusion(s32[256]{0:T(256)S(1)} %iota_add_fusion.1, s32[16384]{0:T(1024)S(1)} %iota_add_fusion, pred[16384]{0:T(1024)(128)(4,1)S(1)} %get-tuple-element.103, pred[16384]{0:T(1024)(128)(4,1)S(1)} %get-tuple-element.104), kind=kLoop, calls=%fused_computation.7 | loop fusion | flops 12582912 | bytes 4293632 | tf_op jit(solution)/shard_map/or | solution.py:185
  34.4 8.3 %all-gather.9.cloned.1.call-done = bf16[1,256,3072]{2,1,0:T(8,128)(2,1)} async-done(((bf16[1,256,768]{2,1,0:T(8,128)(2,1)}), bf16[1,256,3072]{2,1,0:T(8,128)(2,1)}) %all-gather.9.cloned.1.call-update) | async-done | bytes 1572880 | tf_op jit(solution)/shard_map/all_gather | solution.py:94
  49.5 4.3 %fusion.13 = bf16[256,2,384]{2,0,1:T(8,128)(2,1)S(1)} fusion(bf16[3072,2,384]{2,1,0:T(2,128)(2,1)} %param.25, bf16[256,3072]{1,0:T(8,128)(2,1)} %copy-done.1), kind=kOutput, calls=%fused_computation.20 | convolution fusion | flops 1208156160 | bytes 6684672 | tf_op jit(solution)/shard_map/td,dkc->tkc/dot_general | solution.py:125
  53.9 3.1 collective-permute-start.2
  58.6 9.8 %all_gather.15 = bf16[256,512]{1,0:T(8,128)(2,1)S(1)} all-gather(bf16[256,128]{1,0:T(8,128)(2,1)S(1)} %convolution_convert_fusion), channel_id=1, replica_groups=mesh['seq'=32,'mp'=4,'req'=2] {'mp'}, dimensions={1}, use_global_device_ids=true | all-gather | bytes 327680 | tf_op jit(solution)/shard_map/all_gather | solution.py:110
  68.4 2.7 collective-permute-start.3
  75.7 10.7 %all-to-all-start = ((f32[32,3,5,256]{3,1,2,0:T(4,128)}), f32[32,3,5,256]{3,1,2,0:T(4,128)}, u32[]{:S(2)}, u32[]{:S(2)}) async-start(f32[32,3,5,256]{3,1,2,0:T(4,128)} %pad_maximum_fusion), calls=%async_computation | async-start | bytes 1310720 | tf_op jit(solution)/shard_map/all_to_all | solution.py:155
  86.5 2.3 fusion.90
  93.0 8.7 %all-to-all-done = f32[32,3,5,256]{3,1,2,0:T(4,128)} async-done(((f32[32,3,5,256]{3,1,2,0:T(4,128)}), f32[32,3,5,256]{3,1,2,0:T(4,128)}, u32[]{:S(2)}, u32[]{:S(2)}) %all-to-all-start) | async-done | bytes 491552 | tf_op jit(solution)/shard_map/all_to_all | solution.py:155
  124.7 7.0 %all-to-all-start.1 = ((f32[32,3,4,256]{3,2,1,0:T(4,128)}), f32[32,3,4,256]{3,2,1,0:T(4,128)}, u32[]{:S(2)}, u32[]{:S(2)}) async-start(f32[32,3,4,256]{3,2,1,0:T(4,128)} %copy.77), calls=%async_computation.1 | async-start | bytes 786432 | tf_op jit(solution)/shard_map/all_to_all | solution.py:162
  132.0 2.6 fusion.91
  136.3 1.9 copy.79
  148.7 2.5 multiply_reduce_fusion
  151.4 4.6 %constant_dynamic-update-slice_fusion.1 = bf16[16384,256]{0,1:T(8,128)(2,1)} fusion(bf16[8192,256]{0,1:T(8,128)(2,1)} %all-gather.5.cloned.1.call-done), kind=kLoop, calls=%fused_computation.102 | loop fusion | bytes 8388608
  156.0 62.0 %all-gather.7.cloned.1.call-done = bf16[8192,256]{0,1:T(8,128)(2,1)} async-done(((bf16[256,256]{0,1:T(8,128)(2,1)}), bf16[8192,256]{0,1:T(8,128)(2,1)}) %all-gather.7.cloned.1.call-update) | async-done | bytes 4194320 | tf_op jit(solution)/shard_map/all_gather | solution.py:124
  218.0 4.6 %constant_dynamic-update-slice_fusion = bf16[16384,256]{0,1:T(8,128)(2,1)} fusion(bf16[16384,256]{0,1:T(8,128)(2,1)} %constant_dynamic-update-slice_fusion.1, bf16[8192,256]{0,1:T(8,128)(2,1)} %all-gather.7.cloned.1.call-done), kind=kLoop, calls=%fused_computation.101 | loop fusion | bytes 8388608 | tf_op jit(solution)/shard_map/concatenate | solution.py:178
  222.6 17.3 %fusion = (f32[2,256]{1,0:T(2,128)S(1)}, f32[16384,256,2]{1,0,2:T(8,128)}) fusion(pred[256,16384]{0,1:T(8,128)(4,1)} %and_or_fusion, bf16[256,2,64]{2,0,1:T(8,128)(2,1)S(1)} %copy-done.8, bf16[256,2,64]{2,0,1:T(8,128)(2,1)S(1)} %copy-done.7, bf16[16384,256]{0,1:T(8,128)(2,1)} %constant_dynamic-update-slice_fusion), kind=kOutput, calls=%fused_computation.2 | convolution fusion | flops 2172911104 | bytes 42076160 | tf_op jit(solution)/shard_map/qhd,kd->hqk/dot_general | solution.py:187
  239.9 15.7 %fusion.1 = f32[2,256]{1,0:T(2,128)S(1)} fusion(f32[16384,256,2]{1,0,2:T(8,128)} %get-tuple-element.98, f32[2,256]{1,0:T(2,128)S(1)} %broadcast_maximum_fusion, pred[256,16384]{0,1:T(8,128)(4,1)} %and_or_fusion), kind=kLoop, calls=%fused_computation.3 | loop fusion | flops 41942528 | bytes 37752832 | tf_op jit(solution)/shard_map/reduce_sum | solution.py:192
  255.6 17.2 %fusion.27 = bf16[256,2,128]{0,2,1:T(8,128)(2,1)S(1)} fusion(f32[16384,256,2]{1,0,2:T(8,128)} %get-tuple-element.98, f32[2,256]{1,0:T(2,128)S(1)} %broadcast_maximum_fusion, pred[256,16384]{0,1:T(8,128)(4,1)} %and_or_fusion, bf16[16384,256]{0,1:T(8,128)(2,1)} %constant_dynamic-update-slice_fusion, f32[256,2]{0,1:T(2,128)S(1)} %bitcast.367), kind=kOutput, calls=%fused_computation.30 | convolution fusion | flops 2189557760 | bytes 42078208 | tf_op jit(solution)/shard_map/hqk,kd->hqd/dot_general | solution.py:193
  272.8 2.0 fusion.92
  274.9 2.7 convolution_add_fusion
  279.2 42.8 %reduce-scatter.2.cloned.1.call-done = f32[256,768]{1,0:T(8,128)} async-done(((f32[256,3072]{1,0:T(8,128)}), f32[256,768]{1,0:T(8,128)}) %reduce-scatter.2.cloned.1.call-update) | async-done | bytes 786448 | tf_op jit(solution)/shard_map/reduce_scatter | solution.py:204
  322.0 2.0 fusion.40
  (159 shorter events, 62.9 us)
Async XLA Ops:
  7.2 267.7 %copy-start = (bf16[384,3072]{1,0:T(8,128)(2,1)S(1)}, bf16[384,3072]{1,0:T(8,128)(2,1)}, u32[]{:S(2)}) copy-start(bf16[384,3072]{1,0:T(8,128)(2,1)} %param.34) | copy-start | bytes 7077892
  7.2 35.5 %all-gather.9.cloned.1.call-start = ((), (), s32[]{:S(2)}) async-start(), calls=%async_computation.6 | async-start | bytes 1966080 | tf_op jit(solution)/shard_map/all_gather | solution.py:94
  7.9 143.5 %all-gather.5.cloned.1.call-start = ((), (), s32[]{:S(2)}) async-start(), calls=%async_computation.3 | async-start | bytes 4325376 | tf_op jit(solution)/shard_map/all_gather | solution.py:123
  8.9 9.2 %collective-permute-start = (bf16[256,128]{0,1:T(8,128)(2,1)S(1)}, bf16[256,128]{0,1:T(8,128)(2,1)S(1)}, u32[]{:S(2)}, u32[]{:S(2)}) collective-permute-start(bf16[256,128]{0,1:T(8,128)(2,1)S(1)} %bitcast.357), channel_id=1, source_target_pairs={{0,2},{2,0},{4,6},{6,4},{1,3},{3,1},{5,7},{7,5},{8,10},{10,8},{12,... | collective-permute-start | bytes 196616 | tf_op jit(solution)/shard_map/ppermute | solution.py:116
  18.8 28.8 %copy-start.9 = (bf16[3072,3]{0,1:T(4,128)(2,1)S(1)}, bf16[3072,3]{0,1:T(4,128)(2,1)}, u32[]{:S(2)}) copy-start(bf16[3072,3]{0,1:T(4,128)(2,1)} %param.27) | copy-start | bytes 55300
  18.8 28.8 %copy-start.14 = (f32[3]{0:T(128)S(1)}, f32[3]{0:T(128)}, u32[]{:S(2)}) copy-start(f32[3]{0:T(128)} %param.28) | copy-start | bytes 40
  49.5 8.6 %copy-start.2 = (bf16[256,3072]{1,0:T(8,128)(2,1)S(1)}, bf16[256,3072]{1,0:T(8,128)(2,1)}, u32[]{:S(2)}) copy-start(bf16[256,3072]{1,0:T(8,128)(2,1)} %copy-done.1) | copy-start | bytes 4718596
  49.5 8.6 %copy-start.4 = (bf16[3072,128]{1,0:T(8,128)(2,1)S(1)}, bf16[3072,128]{1,0:T(8,128)(2,1)}, u32[]{:S(2)}) copy-start(bf16[3072,128]{1,0:T(8,128)(2,1)} %param.26) | copy-start | bytes 2359300
  49.5 21.7 %copy-start.11 = (bf16[1,3,384]{2,1,0:T(4,128)(2,1)S(1)}, bf16[1,3,384]{2,1,0:T(4,128)(2,1)}, u32[]{:S(2)}) copy-start(bf16[1,3,384]{2,1,0:T(4,128)(2,1)} %param.37) | copy-start | bytes 6916
  53.8 18.6 %copy-start.10 = (bf16[1,3,512]{2,1,0:T(4,128)(2,1)S(1)}, bf16[1,3,512]{2,1,0:T(4,128)(2,1)}, u32[]{:S(2)}) copy-start(bf16[1,3,512]{2,1,0:T(4,128)(2,1)} %param.38) | copy-start | bytes 9220
  53.9 17.3 %collective-permute-start.2 = (bf16[3,384]{1,0:T(4,128)(2,1)S(1)}, bf16[3,384]{1,0:T(4,128)(2,1)S(1)}, u32[]{:S(2)}, u32[]{:S(2)}) collective-permute-start(bf16[3,384]{1,0:T(4,128)(2,1)S(1)} %slice_bitcast_fusion.73), channel_id=1, source_target_pairs={{0,8},{8,16},{16,24},{24,32},{32,40},{40,48},{48,56},{56,64},{64,7... | collective-permute-start | bytes 6920 | tf_op jit(solution)/shard_map/ppermute | solution.py:19
  68.4 6.2 %copy-start.12 = (f32[3]{0:T(128)}, f32[3]{0:T(128)S(1)}, u32[]{:S(2)}) copy-start(f32[3]{0:T(128)S(1)} %exp.54) | copy-start | bytes 40
  68.4 4.0 %collective-permute-start.3 = (bf16[3,512]{1,0:T(4,128)(2,1)S(1)}, bf16[3,512]{1,0:T(4,128)(2,1)S(1)}, u32[]{:S(2)}, u32[]{:S(2)}) collective-permute-start(bf16[3,512]{1,0:T(4,128)(2,1)S(1)} %slice.510), channel_id=1, source_target_pairs={{0,8},{8,16},{16,24},{24,32},{32,40},{40,48},{48,56},{56,64},{64,7... | collective-permute-start | bytes 9224 | tf_op jit(solution)/shard_map/ppermute | solution.py:19
  75.7 26.1 %all-to-all-start = ((f32[32,3,5,256]{3,1,2,0:T(4,128)}), f32[32,3,5,256]{3,1,2,0:T(4,128)}, u32[]{:S(2)}, u32[]{:S(2)}) async-start(f32[32,3,5,256]{3,1,2,0:T(4,128)} %pad_maximum_fusion), calls=%async_computation | async-start | bytes 1310720 | tf_op jit(solution)/shard_map/all_to_all | solution.py:155
  86.4 131.6 %all-gather.7.cloned.1.call-start = ((), (), s32[]{:S(2)}) async-start(), calls=%async_computation.4 | async-start | bytes 4325376 | tf_op jit(solution)/shard_map/all_gather | solution.py:124
  89.1 3.2 copy-start.5
  89.1 3.2 collective-permute-start.1
  124.7 18.9 %all-to-all-start.1 = ((f32[32,3,4,256]{3,2,1,0:T(4,128)}), f32[32,3,4,256]{3,2,1,0:T(4,128)}, u32[]{:S(2)}, u32[]{:S(2)}) async-start(f32[32,3,4,256]{3,2,1,0:T(4,128)} %copy.77), calls=%async_computation.1 | async-start | bytes 786432 | tf_op jit(solution)/shard_map/all_to_all | solution.py:162
  131.7 190.3 %reduce-scatter.2.cloned.1.call-start = ((), (), s32[]{:S(2)}) async-start(), calls=%async_computation.5 | async-start | bytes 3932160 | tf_op jit(solution)/shard_map/reduce_scatter | solution.py:204
  156.0 66.6 %copy-start.7 = (bf16[256,2,64]{2,0,1:T(8,128)(2,1)S(1)}, bf16[256,2,64]{2,0,1:T(8,128)(2,1)}, u32[]{:S(2)}) copy-start(bf16[256,2,64]{2,0,1:T(8,128)(2,1)} %get-tuple-element.49) | copy-start | bytes 196612
  156.0 66.6 %copy-start.8 = (bf16[256,2,64]{2,0,1:T(8,128)(2,1)S(1)}, bf16[256,2,64]{2,0,1:T(8,128)(2,1)}, u32[]{:S(2)}) copy-start(bf16[256,2,64]{2,0,1:T(8,128)(2,1)} %get-tuple-element.50) | copy-start | bytes 196612
  274.9 2.8 copy-start.6
  274.9 3.5 %copy-start.3 = (f32[3,128,256]{2,1,0:T(8,128)S(1)}, f32[3,128,256]{2,1,0:T(8,128)}, u32[]{:S(2)}) copy-start(f32[3,128,256]{2,1,0:T(8,128)} %reshape.277) | copy-start | bytes 1179652
  274.9 3.5 %copy-start.13 = (f32[3]{0:T(128)S(1)}, f32[3]{0:T(128)}, u32[]{:S(2)}) copy-start(f32[3]{0:T(128)} %copy-done.12) | copy-start | bytes 40
  (1 other events, 1.2 us)
Sparse Core Ops, SparseCore 0:
  9.8 32.8 all-gather.8
  45.2 86.1 all-gather.4
  133.8 84.1 all-gather.6
  277.7 44.2 reduce-scatter.1
where the time goes:
time: 332 us; the launch traced here: 331 us
  waiting for transfers between devices  125 us (38%)
  other arithmetic  69.1 us (21%)
  matrix products  55.4 us (17%)
  local copies, waits for them, and re-layouts  28.8 us (9%)
  starting transfers between devices  27.1 us (8%)
  between operations  14.9 us (4%)
  blocking collectives  9.8 us (3%)
    all_gather x1, waiting for transfers between devices, shards(): new_all = lax.all_gather(paired(kv_block), 'seq', axis=0, tiled=True)  62 us
    reduce_scatter x1, waiting for transfers between devices, shards(): summed = lax.psum_scatter(term, 'mp', scatter_dimension=1, tiled=True)  42.8 us
    unnamed x31, other arithmetic  18.3 us
    dot_general x1, matrix products, shards(): jnp.einsum('qhd,kd->hqk', query, piece[:, :HD], preferred_element_type=jn...  17.3 us
    dot_general x1, matrix products, shards(): jnp.einsum('hqk,kd->hqd', weights.astype(jnp.bfloat16), piece[:, HD:2 * H...  17.2 us
    reduce_sum x1, other arithmetic, shards(): total = jnp.sum(weights, axis=-1)  15.7 us
    or x1, other arithmetic, shards(): slot_ok[None, :]  15.6 us
    unnamed x37, local copies, waits for them, and re-layouts  10.8 us
  transfers between devices with their start and end apart: 10, of which 6 were waited for; matrix products, arithmetic and copies ran while one was open for 27% of the time, Pallas kernels for 0%

commit v1 on v0

--- a/solution.py
+++ b/solution.py
@@ -121,7 +121,9 @@
         )
 
     cache_all = lax.all_gather(paired(cache[0]), "seq", axis=0, tiled=True)
-    new_all = lax.all_gather(paired(kv_block), "seq", axis=0, tiled=True)
+    new_all = jnp.concatenate(
+        lax.all_to_all(jnp.stack([paired(kv_block)] * lax.axis_size("seq")), "seq", 0, 0), axis=0
+    )
     inner = jnp.einsum("td,dkc->tkc", normed, w_inner, preferred_element_type=jnp.float32).astype(
         jnp.bfloat16
     )

time: 332 us -> 372 us (1.12)
  waiting for transfers between devices: 125 us -> 162 us
  local copies, waits for them, and re-layouts: 28.8 us -> 33 us
    all_gather x1 -> x0, waiting for transfers between devices: 62 us -> none  [shards(): new_all = lax.all_gather(paired(kv_block), 'seq', axis=0, tiled=True)]
    all_gather x1, waiting for transfers between devices: 0.02 us -> 45 us  [shards(): cache_all = lax.all_gather(paired(cache[0]), 'seq', axis=0, tiled=True)]
    all_to_all x0 -> x1, waiting for transfers between devices: none -> 23.6 us  [shards(): lax.all_to_all(jnp.stack([paired(kv_block)] * lax.axis_size('seq')), 'seq...]
    all_gather x1, waiting for transfers between devices: 8.26 us -> 31.7 us  [shards(): whole = lax.all_gather(own_rows, 'mp', axis=1, tiled=True)]
    all_to_all x0 -> x1, starting transfers between devices: none -> 5.08 us  [shards(): lax.all_to_all(jnp.stack([paired(kv_block)] * lax.axis_size('seq')), 'seq...]
    concatenate x1, local copies, waits for them, and re-layouts: 4.57 us -> 0.43 us  [shards(): piece = jnp.concatenate([cache_all, new_all], axis=0)]
    unnamed x37 -> x49, local copies, waits for them, and re-layouts: 10.8 us -> 13.9 us
  transfers between devices with their start and end apart: 10 -> 10, of which waited for: 6 -> 8; matrix products, arithmetic and copies ran while one was open for 27% -> 20% of each run, Pallas kernels for 0% -> 0%
where the time goes in v1:
time: 372 us; the launch traced here: 371 us
  waiting for transfers between devices  162 us (44%)
  other arithmetic  67.8 us (18%)
  matrix products  52.2 us (14%)
  local copies, waits for them, and re-layouts  33 us (9%)
  starting transfers between devices  29.1 us (8%)
  between operations  16.8 us (5%)
  blocking collectives  9.36 us (3%)
    all_gather x1, waiting for transfers between devices, shards(): cache_all = lax.all_gather(paired(cache[0]), 'seq', axis=0, tiled=True)  45 us
    reduce_scatter x1, waiting for transfers between devices, shards(): summed = lax.psum_scatter(term, 'mp', scatter_dimension=1, tiled=True)  41.4 us
    all_gather x1, waiting for transfers between devices, shards(): whole = lax.all_gather(own_rows, 'mp', axis=1, tiled=True)  31.7 us
    all_to_all x1, waiting for transfers between devices, shards(): lax.all_to_all(jnp.stack([paired(kv_block)] * lax.axis_size('seq')), 'seq...  23.6 us
    unnamed x31, other arithmetic  18.3 us
    dot_general x1, matrix products, shards(): jnp.einsum('hqk,kd->hqd', weights.astype(jnp.bfloat16), piece[:, HD:2 * H...  17.4 us
    dot_general x1, matrix products, shards(): jnp.einsum('qhd,kd->hqk', query, piece[:, :HD], preferred_element_type=jn...  17.2 us
    reduce_sum x1, other arithmetic, shards(): total = jnp.sum(weights, axis=-1)  15.7 us
  transfers between devices with their start and end apart: 10, of which 8 were waited for; matrix products, arithmetic and copies ran while one was open for 20% of the time, Pallas kernels for 0%

profile of v1, /device:TPU:1, one launch (start us, length us, event | category | flops | bytes accessed | tf_op | source)
XLA Modules:
  0.0 370.7 jit_solution(8449012528934889817)
XLA Ops:
  11.8 31.7 %all-gather.6.cloned.1.call-done = bf16[1,256,3072]{2,1,0:T(8,128)(2,1)} async-done(((bf16[1,256,768]{2,1,0:T(8,128)(2,1)}), bf16[1,256,3072]{2,1,0:T(8,128)(2,1)}) %all-gather.6.cloned.1.call-update) | async-done | bytes 1572880 | tf_op jit(solution)/shard_map/all_gather | solution.py:94
  53.8 3.1 collective-permute-start.2
  57.0 9.4 %all_gather.11 = bf16[256,512]{1,0:T(8,128)(2,1)S(1)} all-gather(bf16[256,128]{1,0:T(8,128)(2,1)S(1)} %convolution_convert_fusion), channel_id=1, replica_groups=mesh['seq'=32,'mp'=4,'req'=2] {'mp'}, dimensions={1}, use_global_device_ids=true | all-gather | bytes 327680 | tf_op jit(solution)/shard_map/all_gather | solution.py:110
  66.4 3.1 collective-permute-start.3
  74.0 10.5 %all-to-all-start.1 = ((f32[32,3,5,256]{3,1,2,0:T(4,128)}), f32[32,3,5,256]{3,1,2,0:T(4,128)}, u32[]{:S(2)}, u32[]{:S(2)}) async-start(f32[32,3,5,256]{3,1,2,0:T(4,128)} %pad_maximum_fusion), calls=%async_computation.1 | async-start | bytes 1310720 | tf_op jit(solution)/shard_map/all_to_all | solution.py:157
  88.6 10.6 %all-to-all-done.1 = f32[32,3,5,256]{3,1,2,0:T(4,128)} async-done(((f32[32,3,5,256]{3,1,2,0:T(4,128)}), f32[32,3,5,256]{3,1,2,0:T(4,128)}, u32[]{:S(2)}, u32[]{:S(2)}) %all-to-all-start.1) | async-done | bytes 491552 | tf_op jit(solution)/shard_map/all_to_all | solution.py:157
  122.1 6.8 %all-to-all-start.2 = ((f32[32,3,4,256]{3,2,1,0:T(4,128)}), f32[32,3,4,256]{3,2,1,0:T(4,128)}, u32[]{:S(2)}, u32[]{:S(2)}) async-start(f32[32,3,4,256]{3,2,1,0:T(4,128)} %copy.79), calls=%async_computation.2 | async-start | bytes 786432 | tf_op jit(solution)/shard_map/all_to_all | solution.py:164
  128.9 2.3 fusion.90
  131.6 3.5 collective-permute-done.1
  135.2 4.9 %all-to-all-done.2 = f32[32,3,4,256]{3,2,1,0:T(4,128)} async-done(((f32[32,3,4,256]{3,2,1,0:T(4,128)}), f32[32,3,4,256]{3,2,1,0:T(4,128)}, u32[]{:S(2)}, u32[]{:S(2)}) %all-to-all-start.2) | async-done | bytes 393248 | tf_op jit(solution)/shard_map/all_to_all | solution.py:164
  140.1 2.4 stack.132
  142.5 5.1 %all-to-all-start = ((bf16[32,256,256]{1,2,0:T(8,128)(2,1)}), bf16[32,256,256]{1,2,0:T(8,128)(2,1)}, u32[]{:S(2)}, u32[]{:S(2)}) async-start(bf16[32,256,256]{1,2,0:T(8,128)(2,1)} %stack.132), calls=%async_computation | async-start | bytes 8388608 | tf_op jit(solution)/shard_map/all_to_all | solution.py:125
  149.8 15.5 %and_or_fusion = pred[256,16384]{0,1:T(8,128)(4,1)} fusion(s32[256]{0:T(256)S(1)} %iota_add_fusion.1, s32[16384]{0:T(1024)S(1)} %iota_add_fusion, pred[16384]{0:T(1024)(128)(4,1)S(1)} %get-tuple-element.103, pred[16384]{0:T(1024)(128)(4,1)S(1)} %get-tuple-element.104), kind=kLoop, calls=%fused_computation.7 | loop fusion | flops 12582912 | bytes 4293632 | tf_op jit(solution)/shard_map/or | solution.py:187
  178.9 2.5 multiply_reduce_fusion
  181.6 45.0 %all-gather.4.cloned.1.call-done = bf16[8192,256]{0,1:T(8,128)(2,1)} async-done(((bf16[256,256]{0,1:T(8,128)(2,1)}), bf16[8192,256]{0,1:T(8,128)(2,1)}) %all-gather.4.cloned.1.call-update) | async-done | bytes 4194320 | tf_op jit(solution)/shard_map/all_gather | solution.py:123
  226.6 4.6 %constant_dynamic-update-slice_fusion.1 = bf16[16384,256]{0,1:T(8,128)(2,1)} fusion(bf16[8192,256]{0,1:T(8,128)(2,1)} %all-gather.4.cloned.1.call-done), kind=kLoop, calls=%fused_computation.102 | loop fusion | bytes 8388608
  231.2 23.6 %all-to-all-done = bf16[32,256,256]{1,2,0:T(8,128)(2,1)} async-done(((bf16[32,256,256]{1,2,0:T(8,128)(2,1)}), bf16[32,256,256]{1,2,0:T(8,128)(2,1)}, u32[]{:S(2)}, u32[]{:S(2)}) %all-to-all-start) | async-done | bytes 4194336 | tf_op jit(solution)/shard_map/all_to_all | solution.py:125
  254.8 2.8 copy.90
  259.9 3.2 copy-done.5
  263.1 17.2 %fusion = (f32[2,256]{1,0:T(2,128)S(1)}, f32[16384,256,2]{1,0,2:T(8,128)}) fusion(pred[256,16384]{0,1:T(8,128)(4,1)} %and_or_fusion, bf16[256,2,64]{2,0,1:T(8,128)(2,1)S(1)} %copy-done.11, bf16[256,2,64]{2,0,1:T(8,128)(2,1)S(1)} %copy-done.10, bf16[16384,256]{0,1:T(8,128)(2,1)} %copy-done.5), kind=kOutput, calls=%fused_computation.2 | convolution fusion | flops 2172911104 | bytes 42076160 | tf_op jit(solution)/shard_map/qhd,kd->hqk/dot_general | solution.py:189
  280.4 15.7 %fusion.1 = f32[2,256]{1,0:T(2,128)S(1)} fusion(f32[16384,256,2]{1,0,2:T(8,128)} %get-tuple-element.98, f32[2,256]{1,0:T(2,128)S(1)} %broadcast_maximum_fusion, pred[256,16384]{0,1:T(8,128)(4,1)} %and_or_fusion), kind=kLoop, calls=%fused_computation.3 | loop fusion | flops 41942528 | bytes 37752832 | tf_op jit(solution)/shard_map/reduce_sum | solution.py:194
  296.1 17.4 %fusion.27 = bf16[256,2,128]{0,2,1:T(8,128)(2,1)S(1)} fusion(f32[16384,256,2]{1,0,2:T(8,128)} %get-tuple-element.98, f32[2,256]{1,0:T(2,128)S(1)} %broadcast_maximum_fusion, pred[256,16384]{0,1:T(8,128)(4,1)} %and_or_fusion, bf16[16384,256]{0,1:T(8,128)(2,1)} %copy-done.5, f32[256,2]{0,1:T(2,128)S(1)} %bitcast.370), kind=kOutput, calls=%fused_computation.30 | convolution fusion | flops 2189557760 | bytes 42078208 | tf_op jit(solution)/shard_map/hqk,kd->hqd/dot_general | solution.py:195
  315.5 2.7 convolution_add_fusion
  319.9 41.4 %reduce-scatter.2.cloned.1.call-done = f32[256,768]{1,0:T(8,128)} async-done(((f32[256,3072]{1,0:T(8,128)}), f32[256,768]{1,0:T(8,128)}) %reduce-scatter.2.cloned.1.call-update) | async-done | bytes 786448 | tf_op jit(solution)/shard_map/reduce_scatter | solution.py:206
  (172 shorter events, 68.8 us)
Async XLA Ops:
  8.0 307.5 %copy-start = (bf16[384,3072]{1,0:T(8,128)(2,1)S(1)}, bf16[384,3072]{1,0:T(8,128)(2,1)}, u32[]{:S(2)}) copy-start(bf16[384,3072]{1,0:T(8,128)(2,1)} %param.34) | copy-start | bytes 7077892
  8.0 35.5 %all-gather.6.cloned.1.call-start = ((), (), s32[]{:S(2)}) async-start(), calls=%async_computation.6 | async-start | bytes 1966080 | tf_op jit(solution)/shard_map/all_gather | solution.py:94
  43.5 3.9 %copy-start.20 = (bf16[3072,2,384]{2,1,0:T(2,128)(2,1)S(1)}, bf16[3072,2,384]{2,1,0:T(2,128)(2,1)}, u32[]{:S(2)}) copy-start(bf16[3072,2,384]{2,1,0:T(2,128)(2,1)} %param.25) | copy-start | bytes 14155780
  47.5 4.4 %copy-start.7 = (bf16[3072,128]{1,0:T(8,128)(2,1)S(1)}, bf16[3072,128]{1,0:T(8,128)(2,1)}, u32[]{:S(2)}) copy-start(bf16[3072,128]{1,0:T(8,128)(2,1)} %param.26) | copy-start | bytes 2359300
  48.9 20.6 %copy-start.15 = (bf16[1,3,384]{2,1,0:T(4,128)(2,1)S(1)}, bf16[1,3,384]{2,1,0:T(4,128)(2,1)}, u32[]{:S(2)}) copy-start(bf16[1,3,384]{2,1,0:T(4,128)(2,1)} %param.37) | copy-start | bytes 6916
  48.9 21.8 %copy-start.14 = (bf16[1,3,512]{2,1,0:T(4,128)(2,1)S(1)}, bf16[1,3,512]{2,1,0:T(4,128)(2,1)}, u32[]{:S(2)}) copy-start(bf16[1,3,512]{2,1,0:T(4,128)(2,1)} %param.38) | copy-start | bytes 9220
  53.8 15.7 %collective-permute-start.2 = (bf16[3,384]{1,0:T(4,128)(2,1)S(1)}, bf16[3,384]{1,0:T(4,128)(2,1)S(1)}, u32[]{:S(2)}, u32[]{:S(2)}) collective-permute-start(bf16[3,384]{1,0:T(4,128)(2,1)S(1)} %slice_bitcast_fusion.73), channel_id=1, source_target_pairs={{0,8},{8,16},{16,24},{24,32},{32,40},{40,48},{48,56},{56,64},{64,7... | collective-permute-start | bytes 6920 | tf_op jit(solution)/shard_map/ppermute | solution.py:19
  66.3 6.6 %copy-start.16 = (f32[3]{0:T(128)}, f32[3]{0:T(128)S(1)}, u32[]{:S(2)}) copy-start(f32[3]{0:T(128)S(1)} %exp.54) | copy-start | bytes 40
  66.4 4.4 %collective-permute-start.3 = (bf16[3,512]{1,0:T(4,128)(2,1)S(1)}, bf16[3,512]{1,0:T(4,128)(2,1)S(1)}, u32[]{:S(2)}, u32[]{:S(2)}) collective-permute-start(bf16[3,512]{1,0:T(4,128)(2,1)S(1)} %slice.510), channel_id=1, source_target_pairs={{0,8},{8,16},{16,24},{24,32},{32,40},{40,48},{48,56},{56,64},{64,7... | collective-permute-start | bytes 9224 | tf_op jit(solution)/shard_map/ppermute | solution.py:19
  70.7 13.9 %copy-start.12 = (bf16[1,256,128]{2,1,0:T(8,128)(2,1)S(1)}, bf16[1,256,128]{2,1,0:T(8,128)(2,1)}, u32[]{:S(2)}) copy-start(bf16[1,256,128]{2,1,0:T(8,128)(2,1)} %param.35) | copy-start | bytes 196612
  74.0 25.2 %all-to-all-start.1 = ((f32[32,3,5,256]{3,1,2,0:T(4,128)}), f32[32,3,5,256]{3,1,2,0:T(4,128)}, u32[]{:S(2)}, u32[]{:S(2)}) async-start(f32[32,3,5,256]{3,1,2,0:T(4,128)} %pad_maximum_fusion), calls=%async_computation.1 | async-start | bytes 1310720 | tf_op jit(solution)/shard_map/all_to_all | solution.py:157
  84.6 142.1 %all-gather.4.cloned.1.call-start = ((), (), s32[]{:S(2)}) async-start(), calls=%async_computation.4 | async-start | bytes 4325376 | tf_op jit(solution)/shard_map/all_gather | solution.py:123
  84.7 3.2 collective-permute-start
  122.1 18.0 %all-to-all-start.2 = ((f32[32,3,4,256]{3,2,1,0:T(4,128)}), f32[32,3,4,256]{3,2,1,0:T(4,128)}, u32[]{:S(2)}, u32[]{:S(2)}) async-start(f32[32,3,4,256]{3,2,1,0:T(4,128)} %copy.79), calls=%async_computation.2 | async-start | bytes 786432 | tf_op jit(solution)/shard_map/all_to_all | solution.py:164
  131.5 3.6 copy-start.8
  131.5 3.6 collective-permute-start.1
  142.5 5.3 %copy-start.18 = (bf16[384]{0:T(512)(128)(2,1)S(1)}, bf16[384]{0:T(512)(128)(2,1)}, u32[]{:S(2)}) copy-start(bf16[384]{0:T(512)(128)(2,1)} %param.33) | copy-start | bytes 2308
  142.5 112.3 %all-to-all-start = ((bf16[32,256,256]{1,2,0:T(8,128)(2,1)}), bf16[32,256,256]{1,2,0:T(8,128)(2,1)}, u32[]{:S(2)}, u32[]{:S(2)}) async-start(bf16[32,256,256]{1,2,0:T(8,128)(2,1)} %stack.132), calls=%async_computation | async-start | bytes 8388608 | tf_op jit(solution)/shard_map/all_to_all | solution.py:125
  147.6 213.7 %reduce-scatter.2.cloned.1.call-start = ((), (), s32[]{:S(2)}) async-start(), calls=%async_computation.5 | async-start | bytes 3932160 | tf_op jit(solution)/shard_map/reduce_scatter | solution.py:206
  147.8 17.5 %copy-start.2 = (bf16[256,3072]{1,0:T(8,128)(2,1)S(1)}, bf16[256,3072]{1,0:T(8,128)(2,1)}, u32[]{:S(2)}) copy-start(bf16[256,3072]{1,0:T(8,128)(2,1)} %copy-done.1) | copy-start | bytes 4718596
  147.8 17.5 %copy-start.6 = (bf16[3072,256]{1,0:T(8,128)(2,1)S(1)}, bf16[3072,256]{1,0:T(8,128)(2,1)}, u32[]{:S(2)}) copy-start(bf16[3072,256]{1,0:T(8,128)(2,1)} %param.22) | copy-start | bytes 4718596
  254.8 4.6 %copy-start.4 = (bf16[16384,256]{0,1:T(8,128)(2,1)S(1)}, bf16[16384,256]{0,1:T(8,128)(2,1)}, u32[]{:S(2)}) copy-start(bf16[16384,256]{0,1:T(8,128)(2,1)} %constant_dynamic-update-slice_fusion.1) | copy-start | bytes 25165828
  259.4 3.7 copy-start.10
  259.4 3.7 copy-start.11
  (7 other events, 19.9 us)
Sparse Core Ops, SparseCore 0:
  10.7 32.8 all-gather.5
  318.4 42.8 reduce-scatter.1
Sparse Core Ops, SparseCore 1:
  88.7 137.9 all-gather.3
